TPU v7x, 32 devices: a whole 2x2x4 slice. The times are simulated.
32 devices in a mesh: dp: 8 (over z, x), mp: 4 (over y, core).
Axes of the slice: x: 2, y: 2, z: 4, core: 2. Of those that a mesh axis runs over, the one named last changes fastest.
Arguments:
- features: bfloat16 [8192, 1024], P('dp'), may hold values from -6 to 6
- out_grads: bfloat16 [8192, 4, 1024], P('dp', None, 'mp'), may hold values from -0.0625 to 0.0625
- norm_grads: float32 [8, 2048], P('dp'), may hold values from -2 to 2
- owners: int32 [5], replicated, may hold values from 0 to 7, as said below
- moment1: float32 [4, 1024, 1024], P(None, 'dp', 'mp'), may hold values from -6 to 6
- moment2: float32 [4, 1024, 1024], P(None, 'dp', 'mp'), may hold values from 0.1 to 10
- left_stats: float32 [4, 1024, 1024], P(None, 'dp', 'mp'), may hold values from -1024 to 1024, as said below
- right_stats: float32 [4, 1024, 1024], P(None, 'dp', 'mp'), may hold values from -1024 to 1024, as said below
- left_basis: float32 [4, 1024, 1024], P(None, 'dp', 'mp'), may hold values from -1 to 2
- right_basis: float32 [4, 1024, 1024], P(None, 'dp', 'mp'), may hold values from -1 to 2
- norm_m: float32 [2048], P('dp'), may hold values from -6 to 6
- norm_v: float32 [2048], P('dp'), may hold values from 0.1 to 10
Outputs:
- new_moment1: float32 [4, 1024, 1024], P(None, 'dp', 'mp')
- new_moment2: float32 [4, 1024, 1024], P(None, 'dp', 'mp')
- new_left_stats: float32 [4, 1024, 1024], P(None, 'dp', 'mp')
- new_right_stats: float32 [4, 1024, 1024], P(None, 'dp', 'mp')
- new_left_basis: float32 [4, 1024, 1024], P(None, 'dp', 'mp')
- new_right_basis: float32 [4, 1024, 1024], P(None, 'dp', 'mp')
- update_slots: bfloat16 [8, 1024, 1024], P('dp', None, 'mp')
- new_norm_m: float32 [2048], P('dp')
- new_norm_v: float32 [2048], P('dp')
- norm_slots: float32 [8, 2048], P('dp')
Inputs may be any that keep to these rules, and one draw needn't show every extreme that they name: `owners`: the first 4 entries are distinct, so a dp index owns at most one tile; the last entry may equal any of them. `left_stats`: each tile of statistics is symmetric. `right_stats`: each tile of statistics is symmetric.
All inputs are finite; a program needn't handle non-finite values.
Results may differ from a plain program's by a relative error of at most 0.0072.
Values may be sent and summed in bfloat16 or wider, within the bound.
A program may use at most 128 MiB of HBM per device.

v0:
```python
import jax
import jax.numpy as jnp
from jax import lax
from jax.sharding import PartitionSpec as P

FIX_ONE = 1.0 - 0.9**10
FIX_TWO = 1.0 - 0.95**10
BF = jnp.bfloat16
F32 = jnp.float32


def contract(left, right, left_dim, right_dim):
    return lax.dot_general(
        left, right, (((left_dim,), (right_dim,)), ((), ())), preferred_element_type=F32
    )


def to_tile(blocks):
    out = lax.all_to_all(blocks, "mp", split_axis=1, concat_axis=1, tiled=True)
    k, n, r, c = out.shape
    return out.transpose(0, 2, 1, 3).reshape(k, r, n * c)


def to_home(rows, n):
    k, r, c = rows.shape
    out = rows.reshape(k, r, n, c // n).transpose(0, 2, 1, 3)
    return lax.all_to_all(out, "mp", split_axis=1, concat_axis=1, tiled=True)


def gather_rows(rows):
    return lax.all_gather(rows, "dp", axis=0, tiled=True)


def normalize(power):
    wide = power.astype(F32)
    return lax.rsqrt(jnp.sum(wide * wide, axis=0, keepdims=True) + 1e-06)


def shards(
    features,
    out_grads,
    norm_grads,
    owners,
    moment1,
    moment2,
    left_stats,
    right_stats,
    left_basis,
    right_basis,
    norm_m,
    norm_v,
):
    dp = lax.axis_size("dp")
    tiles, slab, width = moment1.shape
    full = slab * dp
    me = lax.axis_index("dp")
    row0 = me * slab
    narrow = to_tile(jnp.stack([left_basis, right_basis, left_stats, right_stats]).astype(BF))
    left_full = gather_rows(narrow[0])
    right_full = gather_rows(narrow[1])
    flat = out_grads.reshape(out_grads.shape[0], tiles * width)
    partial = contract(features, flat, 0, 0).astype(BF).reshape(dp, slab, tiles * width)
    parts = lax.all_to_all(partial, "dp", split_axis=0, concat_axis=0, tiled=True)
    grad_home = jnp.sum(parts.astype(F32), axis=0).astype(BF)
    grad_home = grad_home.reshape(slab, tiles, width).transpose(1, 0, 2)
    grad_rows = to_tile(grad_home[None])[0]
    grad_full = gather_rows(grad_rows)
    wide = to_tile(jnp.stack([moment1, moment2]))
    prod_l = contract(grad_rows, grad_full, 1, 1)
    grad_cols = lax.dynamic_slice_in_dim(grad_full, row0, slab, 1)
    prod_r = contract(grad_cols, grad_full, 0, 0)
    stats_l = (0.95 * narrow[2].astype(F32) + 0.05 * prod_l).astype(BF)
    stats_r = (0.95 * narrow[3].astype(F32) + 0.05 * prod_r).astype(BF)
    power_l = contract(stats_l, left_full, 1, 0).astype(BF)
    power_r = contract(stats_r, right_full, 1, 0).astype(BF)
    power_l_full = gather_rows(power_l)
    power_r_full = gather_rows(power_r)
    left_cols = lax.dynamic_slice_in_dim(left_full, row0, slab, 1)
    half = contract(left_cols, grad_full, 0, 0).astype(BF)
    rotated = contract(half, right_full, 1, 0)
    tile_one = 0.9 * wide[0] + 0.1 * rotated
    tile_two = 0.95 * wide[1] + 0.05 * rotated * rotated
    direction = (tile_one / FIX_ONE / (jnp.sqrt(tile_two / FIX_TWO) + 1e-08)).astype(BF)
    back = contract(direction, right_full, 1, 1).astype(BF)
    back_full = gather_rows(back)
    home1 = to_home(jnp.stack([rotated, prod_l, prod_r]).astype(BF), tiles).astype(F32)
    new_one = 0.9 * moment1 + 0.1 * home1[0]
    new_two = 0.95 * moment2 + 0.05 * home1[0] * home1[0]
    new_sl = 0.95 * left_stats + 0.05 * home1[1]
    new_sr = 0.95 * right_stats + 0.05 * home1[2]
    update = contract(narrow[0], back_full, 1, 0).astype(BF)

    def refine(power_full, power_rows):
        scale = normalize(power_full)
        iter_full = (power_full.astype(F32) * scale).astype(BF)
        iter_rows = (power_rows.astype(F32) * scale).astype(BF)
        gram = contract(iter_rows, iter_full, 1, 1).astype(BF)
        return 1.5 * iter_rows.astype(F32) - 0.5 * contract(gram, iter_full, 1, 0)

    new_l = refine(power_l_full, power_l)
    new_r = refine(power_r_full, power_r)
    home2 = to_home(jnp.stack([new_l.astype(BF), new_r.astype(BF), update]), tiles)
    new_bl = home2[0].astype(F32)
    new_br = home2[1].astype(F32)
    slot_of = jnp.arange(dp, dtype=jnp.int32)[:, None, None]
    slots = jnp.zeros((dp, slab, width), BF)
    for n in range(tiles):
        slots = jnp.where(slot_of == owners[n], home2[2, n][None], slots)
    update_slot = lax.all_to_all(slots, "dp", split_axis=0, concat_axis=0, tiled=True)
    update_slot = update_slot.reshape(1, full, width)
    norm_parts = norm_grads.reshape(dp, norm_m.shape[0])
    norm_parts = lax.all_to_all(norm_parts, "dp", split_axis=0, concat_axis=0, tiled=True)
    norm_total = jnp.sum(norm_parts, axis=0)
    new_nm = 0.9 * norm_m + 0.1 * norm_total
    new_nv = 0.95 * norm_v + 0.05 * norm_total * norm_total
    norm_step = new_nm / FIX_ONE / (jnp.sqrt(new_nv / FIX_TWO) + 1e-08)
    to_owner = (jnp.arange(dp, dtype=jnp.int32) == owners[tiles])[:, None]
    norm_out = jnp.where(to_owner, norm_step[None], 0.0)
    norm_slot = lax.all_to_all(norm_out, "dp", split_axis=0, concat_axis=0, tiled=True)
    norm_slot = norm_slot.reshape(1, -1)
    return (
        new_one,
        new_two,
        new_sl,
        new_sr,
        new_bl,
        new_br,
        update_slot,
        new_nm,
        new_nv,
        norm_slot,
    )


def solution(mesh):
    in_specs = (
        P("dp", None),
        P("dp", None, "mp"),
        P("dp", None),
        P(),
        P(None, "dp", "mp"),
        P(None, "dp", "mp"),
        P(None, "dp", "mp"),
        P(None, "dp", "mp"),
        P(None, "dp", "mp"),
        P(None, "dp", "mp"),
        P("dp"),
        P("dp"),
    )
    out_specs = (
        P(None, "dp", "mp"),
        P(None, "dp", "mp"),
        P(None, "dp", "mp"),
        P(None, "dp", "mp"),
        P(None, "dp", "mp"),
        P(None, "dp", "mp"),
        P("dp", None, "mp"),
        P("dp"),
        P("dp"),
        P("dp", None),
    )
    return jax.shard_map(shards, mesh=mesh, in_specs=in_specs, out_specs=out_specs, check_vma=False)
```

profile of v0, /device:TPU:0, one launch (start us, length us, event | category | flops | bytes accessed | tf_op | source)
XLA Modules:
  0.0 443.4 jit_solution(10692234722072050169)
XLA Ops:
  7.2 2.2 copy.122
  9.5 2.4 convolution_convert_fusion
  11.9 55.4 %all_to_all.50 = bf16[8,128,1024]{2,1,0:T(8,128)(2,1)} all-to-all(bf16[8,128,1024]{2,1,0:T(8,128)(2,1)S(1)} %bitcast.115), channel_id=1, replica_groups=mesh['dp'=8,'mp'=4] {'dp'}, dimensions={0} | all-to-all | bytes 4194304 | tf_op jit(solution)/shard_map/all_to_all | solution.py:63
  67.3 2.0 reduce_sum.39
  70.2 1.1 copy.98
  71.3 9.1 %all_to_all.51 = bf16[1,4,128,256]{3,2,0,1:T(8,128)(2,1)} all-to-all(bf16[1,4,128,256]{3,2,0,1:T(8,128)(2,1)S(1)} %copy.98), channel_id=1, replica_groups=mesh['dp'=8,'mp'=4] {'mp'}, dimensions={1} | all-to-all | bytes 524288 | tf_op jit(solution)/shard_map/all_to_all | solution.py:19
  80.4 1.8 copy.99
  82.6 1.2 copy.93
  83.8 1.2 copy.92
  85.2 16.9 %all_to_all.52 = bf16[4,4,128,256]{2,3,0,1:T(8,128)(2,1)S(1)} all-to-all(bf16[4,4,128,256]{2,3,0,1:T(8,128)(2,1)S(1)} %pad_maximum_fusion), channel_id=1, replica_groups=mesh['dp'=8,'mp'=4] {'mp'}, dimensions={1} | all-to-all | bytes 2097152 | tf_op jit(solution)/shard_map/all_to_all | solution.py:19
  104.8 1.2 copy.117
  106.1 24.6 %all-gather.9.cloned.1.call-done = bf16[1024,1024]{0,1:T(8,128)(2,1)} async-done(((bf16[128,1024]{0,1:T(8,128)(2,1)}), bf16[1024,1024]{0,1:T(8,128)(2,1)}) %all-gather.9.cloned.1.call-update) | async-done | bytes 2097168 | tf_op jit(solution)/shard_map/all_gather | solution.py:31
  130.7 3.4 fusion.85
  134.1 47.8 %all-gather.11.cloned.1.call-done = bf16[1024,1024]{0,1:T(8,128)(2,1)} async-done(((bf16[128,1024]{0,1:T(8,128)(2,1)}), bf16[1024,1024]{0,1:T(8,128)(2,1)}) %all-gather.11.cloned.1.call-update) | async-done | bytes 2097168 | tf_op jit(solution)/shard_map/all_gather | solution.py:31
  181.8 3.3 convolution_convert_fusion.3
  185.5 2.8 fusion.86
  188.2 44.8 %all-gather.7.cloned.1.call-done = bf16[1024,1024]{0,1:T(8,128)(2,1)} async-done(((bf16[128,1024]{0,1:T(8,128)(2,1)}), bf16[1024,1024]{0,1:T(8,128)(2,1)}) %all-gather.7.cloned.1.call-update) | async-done | bytes 2097168 | tf_op jit(solution)/shard_map/all_gather | solution.py:31
  233.0 3.1 convolution_convert_fusion.4
  236.2 1.2 copy.108
  237.4 1.2 copy.109
  238.8 17.0 %all_to_all.53 = f32[2,4,128,256]{2,3,0,1:T(8,128)S(1)} all-to-all(f32[2,4,128,256]{2,3,0,1:T(8,128)S(1)} %pad_maximum_fusion.1), channel_id=1, replica_groups=mesh['dp'=8,'mp'=4] {'mp'}, dimensions={1} | all-to-all | bytes 2097152 | tf_op jit(solution)/shard_map/all_to_all | solution.py:19
  257.1 4.8 %fusion.87 = (bf16[128,1024]{1,0:T(8,128)(2,1)}, f32[128,1024]{1,0:T(8,128)}) fusion(bf16[1024,1024]{0,1:T(8,128)(2,1)} %all-gather.11.cloned.1.call-done, bf16[1024,1024]{0,1:T(8,128)(2,1)} %all-gather.9.cloned.1.call-done, bf16[1024,1024]{0,1:T(8,128)(2,1)} %all-gather.7.cloned.1.call-done, s32[]{:T(128)S(6)} %select_n.28), kind=kOutput, calls=%fused_computation.109 | convolution fusion | flops 537133056 | bytes 5242884 | tf_op jit(solution)/shard_map/dot_general | solution.py:13
  261.9 3.1 convolution_convert_fusion.2
  265.1 3.5 all-to-all-start.7
  269.9 5.2 %all-to-all-done.7 = f32[8,1,256]{2,1,0:T(1,128)S(1)} async-done(((f32[8,1,256]{2,1,0:T(1,128)}), f32[8,1,256]{2,1,0:T(1,128)S(1)}, u32[]{:S(2)}, u32[]{:S(2)}) %all-to-all-start.7) | async-done | bytes 8224 | tf_op jit(solution)/shard_map/all_to_all | solution.py:112
  276.4 3.5 all-to-all-start.8
  280.0 3.1 all-gather.15.cloned.1.call-done
  283.1 2.1 fusion.2
  285.1 3.5 fusion.24
  288.9 43.8 %all-gather.13.cloned.1.call-done = bf16[1024,1024]{1,0:T(8,128)(2,1)} async-done(((bf16[128,1024]{1,0:T(8,128)(2,1)}), bf16[1024,1024]{1,0:T(8,128)(2,1)}) %all-gather.13.cloned.1.call-update) | async-done | bytes 2097168 | tf_op jit(solution)/shard_map/all_gather | solution.py:31
  332.7 2.1 fusion
  334.8 3.5 fusion.27
  338.5 44.4 %all-gather.17.cloned.1.call-done = bf16[1024,1024]{1,0:T(8,128)(2,1)} async-done(((bf16[128,1024]{1,0:T(8,128)(2,1)}), bf16[1024,1024]{1,0:T(8,128)(2,1)}) %all-gather.17.cloned.1.call-update) | async-done | bytes 2097168 | tf_op jit(solution)/shard_map/all_gather | solution.py:31
  382.9 2.1 convolution_convert_fusion.1
  386.2 3.6 all-to-all-start.5
  389.8 1.8 stack.58
  391.6 1.7 copy.100
  394.2 1.7 copy.102
  396.1 2.0 maximum_bitcast_fusion
  398.1 3.3 all-to-all-done.5
  401.4 4.2 all-to-all-start.3
  405.6 1.3 iota_compare_fusion.1
  406.9 1.2 iota_compare_fusion.3
  409.2 8.1 %all-to-all-done.3 = bf16[3,4,128,256]{3,2,0,1:T(8,128)(2,1)} async-done(((bf16[3,4,128,256]{3,2,0,1:T(8,128)(2,1)}), bf16[3,4,128,256]{3,2,0,1:T(8,128)(2,1)}, u32[]{:S(2)}, u32[]{:S(2)}) %all-to-all-start.3) | async-done | bytes 786464 | tf_op jit(solution)/shard_map/all_to_all | solution.py:27
  417.3 3.5 all-to-all-start.6
  420.8 1.4 convert_element_type.101
  422.5 1.5 fusion.48
  425.1 10.1 %all-to-all-done.6 = bf16[8,128,256]{2,1,0:T(8,128)(2,1)S(1)} async-done(((bf16[8,128,256]{2,1,0:T(8,128)(2,1)}), bf16[8,128,256]{2,1,0:T(8,128)(2,1)S(1)}, u32[]{:S(2)}, u32[]{:S(2)}) %all-to-all-start.6) | async-done | bytes 524320 | tf_op jit(solution)/shard_map/all_to_all | solution.py:109
  (84 shorter events, 15.1 us)
Async XLA Ops:
  7.2 2.3 copy-start
  7.2 123.5 %all-gather.9.cloned.1.call-start = ((), (), s32[]{:S(2)}) async-start(), calls=%async_computation.10 | async-start | bytes 2359296 | tf_op jit(solution)/shard_map/all_gather | solution.py:31
  67.3 14.9 %copy-start.4 = (f32[4,128,256]{2,1,0:T(8,128)S(1)}, f32[4,128,256]{2,1,0:T(8,128)}, u32[]{:S(2)}) copy-start(f32[4,128,256]{2,1,0:T(8,128)} %param.19) | copy-start | bytes 1572868
  69.3 13.1 %copy-start.6 = (f32[4,128,256]{2,1,0:T(8,128)S(1)}, f32[4,128,256]{2,1,0:T(8,128)}, u32[]{:S(2)}) copy-start(f32[4,128,256]{2,1,0:T(8,128)} %param.18) | copy-start | bytes 1572868
  82.2 99.7 %all-gather.11.cloned.1.call-start = ((), (), s32[]{:S(2)}) async-start(), calls=%async_computation.11 | async-start | bytes 2359296 | tf_op jit(solution)/shard_map/all_gather | solution.py:31
  103.0 130.1 %all-gather.7.cloned.1.call-start = ((), (), s32[]{:S(2)}) async-start(), calls=%async_computation.9 | async-start | bytes 2359296 | tf_op jit(solution)/shard_map/all_gather | solution.py:31
  103.7 179.4 %all-gather.15.cloned.1.call-start = ((), (), s32[]{:S(2)}) async-start(), calls=%async_computation.13 | async-start | bytes 2359296 | tf_op jit(solution)/shard_map/all_gather | solution.py:31
  134.0 51.2 %copy-start.3 = (f32[1,128,4,256]{1,3,2,0:T(8,128)S(1)}, f32[1,128,4,256]{1,3,2,0:T(8,128)}, u32[]{:S(2)}) copy-start(f32[1,128,4,256]{1,3,2,0:T(8,128)} %get-tuple-element.17) | copy-start | bytes 1572868
  181.8 3.6 copy-start.1
  185.2 147.5 %all-gather.13.cloned.1.call-start = ((), (), s32[]{:S(2)}) async-start(), calls=%async_computation.12 | async-start | bytes 2359296 | tf_op jit(solution)/shard_map/all_gather | solution.py:31
  236.2 146.7 %all-gather.17.cloned.1.call-start = ((), (), s32[]{:S(2)}) async-start(), calls=%async_computation.14 | async-start | bytes 2359296 | tf_op jit(solution)/shard_map/all_gather | solution.py:31
  257.1 4.8 %copy-start.14 = (f32[128,1024]{1,0:T(8,128)S(1)}, f32[128,1024]{1,0:T(8,128)}, u32[]{:S(2)}) copy-start(f32[128,1024]{1,0:T(8,128)} %copy.118) | copy-start | bytes 1572868
  261.9 6.7 %copy-start.15 = (s32[5]{0:T(128)S(1)}, s32[5]{0:T(128)}, u32[]{:S(2)}) copy-start(s32[5]{0:T(128)} %param.15) | copy-start | bytes 64
  261.9 13.3 %copy-start.16 = (f32[256]{0:T(256)S(1)}, f32[256]{0:T(256)}, u32[]{:S(2)}) copy-start(f32[256]{0:T(256)} %param.23) | copy-start | bytes 3076
  261.9 13.3 %copy-start.17 = (f32[256]{0:T(256)S(1)}, f32[256]{0:T(256)}, u32[]{:S(2)}) copy-start(f32[256]{0:T(256)} %param.22) | copy-start | bytes 3076
  265.1 20.1 %copy-start.12 = (bf16[128,1024]{1,0:T(8,128)(2,1)S(1)}, bf16[128,1024]{1,0:T(8,128)(2,1)}, u32[]{:S(2)}) copy-start(bf16[128,1024]{1,0:T(8,128)(2,1)} %convolution_convert_fusion.3) | copy-start | bytes 786436
  265.1 10.1 %all-to-all-start.7 = ((f32[8,1,256]{2,1,0:T(1,128)}), f32[8,1,256]{2,1,0:T(1,128)S(1)}, u32[]{:S(2)}, u32[]{:S(2)}) async-start(f32[8,1,256]{2,1,0:T(1,128)} %bitcast.38), calls=%async_computation.7 | async-start | bytes 16384 | tf_op jit(solution)/shard_map/all_to_all | solution.py:112
  276.4 109.7 %all-to-all-start.8 = ((f32[8,1,256]{2,1,0:T(1,128)}), f32[8,1,256]{2,1,0:T(1,128)S(1)}, u32[]{:S(2)}, u32[]{:S(2)}) async-start(f32[8,1,256]{2,1,0:T(1,128)} %broadcast_select_fusion), calls=%async_computation.8 | async-start | bytes 16384 | tf_op jit(solution)/shard_map/all_to_all | solution.py:119
  288.6 46.1 %copy-start.13 = (bf16[128,1024]{1,0:T(8,128)(2,1)S(1)}, bf16[128,1024]{1,0:T(8,128)(2,1)}, u32[]{:S(2)}) copy-start(bf16[128,1024]{1,0:T(8,128)(2,1)} %convolution_convert_fusion.4) | copy-start | bytes 786436
  334.7 48.1 %copy-start.2 = (bf16[1,128,4,256]{1,3,2,0:T(8,128)(2,1)S(1)}, bf16[1,128,4,256]{1,3,2,0:T(8,128)(2,1)}, u32[]{:S(2)}) copy-start(bf16[1,128,4,256]{1,3,2,0:T(8,128)(2,1)} %get-tuple-element.21) | copy-start | bytes 786436
  385.2 8.2 %copy-start.10 = (bf16[128,1024]{1,0:T(8,128)(2,1)S(1)}, bf16[128,1024]{1,0:T(8,128)(2,1)}, u32[]{:S(2)}) copy-start(bf16[128,1024]{1,0:T(8,128)(2,1)} %get-tuple-element.34) | copy-start | bytes 786436
  386.2 9.7 %copy-start.11 = (bf16[128,1024]{1,0:T(8,128)(2,1)S(1)}, bf16[128,1024]{1,0:T(8,128)(2,1)}, u32[]{:S(2)}) copy-start(bf16[128,1024]{1,0:T(8,128)(2,1)} %get-tuple-element.36) | copy-start | bytes 786436
  386.2 15.2 %all-to-all-start.5 = ((bf16[3,4,128,256]{3,2,0,1:T(8,128)(2,1)}), bf16[3,4,128,256]{3,2,0,1:T(8,128)(2,1)S(1)}, u32[]{:S(2)}, u32[]{:S(2)}) async-start(bf16[3,4,128,256]{3,2,0,1:T(8,128)(2,1)} %maximum_bitcast_fusion.1), calls=%async_computation.5 | async-start | bytes 1572864 | tf_op jit(solution)/shard_map/all_to_all | solution.py:27
  401.4 15.9 %all-to-all-start.3 = ((bf16[3,4,128,256]{3,2,0,1:T(8,128)(2,1)}), bf16[3,4,128,256]{3,2,0,1:T(8,128)(2,1)}, u32[]{:S(2)}, u32[]{:S(2)}) async-start(bf16[3,4,128,256]{3,2,0,1:T(8,128)(2,1)} %maximum_bitcast_fusion), calls=%async_computation.3 | async-start | bytes 1572864 | tf_op jit(solution)/shard_map/all_to_all | solution.py:27
  417.3 17.9 %all-to-all-start.6 = ((bf16[8,128,256]{2,1,0:T(8,128)(2,1)}), bf16[8,128,256]{2,1,0:T(8,128)(2,1)S(1)}, u32[]{:S(2)}, u32[]{:S(2)}) async-start(bf16[8,128,256]{2,1,0:T(8,128)(2,1)} %select_select_fusion), calls=%async_computation.6 | async-start | bytes 1048576 | tf_op jit(solution)/shard_map/all_to_all | solution.py:109
  420.8 1.5 copy-start.5
  420.8 1.5 copy-start.7
  420.8 1.6 copy-start.8
  420.8 1.7 copy-start.9
Sparse Core Ops, SparseCore 0:
  82.3 48.3 all-gather.8
  133.3 48.5 all-gather.10
  184.5 48.5 all-gather.6
  235.6 47.4 all-gather.14
  285.0 47.5 all-gather.12
  335.2 47.6 all-gather.16
where the time goes:
time: 445 us; the launch traced here: 443 us
  waiting for transfers between devices  236 us (53%)
  blocking collectives  98.3 us (22%)
  matrix products  32 us (7%)
  local copies, waits for them, and re-layouts  24.2 us (5%)
  other arithmetic  20 us (4%)
  starting transfers between devices  18.5 us (4%)
  between operations  14.6 us (3%)
    all_gather x6, waiting for transfers between devices, gather_rows(): return lax.all_gather(rows, 'dp', axis=0, tiled=True)  208 us
    all_to_all x1, blocking collectives, shards(): lax.all_to_all(partial, 'dp', split_axis=0, concat_axis=0, tiled=True)  55.4 us
    all_to_all x3, blocking collectives, to_tile(): out = lax.all_to_all(blocks, 'mp', split_axis=1, concat_axis=1, tiled=True)  42.9 us
    dot_general x10, matrix products, contract(): lax.dot_general(left, right, (((left_dim,), (right_dim,)), ((), ())), pre...  32 us
    all_to_all x2, waiting for transfers between devices, to_home(): return lax.all_to_all(out, 'mp', split_axis=1, concat_axis=1, tiled=True)  11.3 us
    all_to_all x1, waiting for transfers between devices, shards(): lax.all_to_all(slots, 'dp', split_axis=0, concat_axis=0, tiled=True)  10.1 us
    unnamed x45, local copies, waits for them, and re-layouts  9.22 us
  transfers between devices with their start and end apart: 11, of which 10 were waited for; matrix products, arithmetic and copies ran while one was open for 14% of the time, Pallas kernels for 0%

commit v1 on v0

--- a/solution.py
+++ b/solution.py
@@ -2,6 +2,7 @@
 import jax.numpy as jnp
 from jax import lax
 from jax.sharding import PartitionSpec as P
+from jax.lax import all_to_all, axis_size
 
 FIX_ONE = 1.0 - 0.9**10
 FIX_TWO = 1.0 - 0.95**10
@@ -24,7 +25,9 @@
 def to_home(rows, n):
     k, r, c = rows.shape
     out = rows.reshape(k, r, n, c // n).transpose(0, 2, 1, 3)
-    return lax.all_to_all(out, "mp", split_axis=1, concat_axis=1, tiled=True)
+    return jnp.concatenate(
+        all_to_all(jnp.stack(jnp.split(out, axis_size("mp"), axis=1), 0), "mp", 0, 0), 1
+    )
 
 
 def gather_rows(rows):

time: 445 us -> 445 us (level)
  transfers between devices with their start and end apart: 11 -> 11, of which waited for: 10 -> 10; matrix products, arithmetic and copies ran while one was open for 14% -> 15% of each run, Pallas kernels for 0% -> 0%
where the time goes in v1:
time: 445 us; the launch traced here: 444 us
  waiting for transfers between devices  236 us (53%)
  blocking collectives  98.3 us (22%)
  matrix products  31.9 us (7%)
  local copies, waits for them, and re-layouts  24.3 us (5%)
  other arithmetic  20.3 us (5%)
  starting transfers between devices  18.5 us (4%)
  between operations  14.6 us (3%)
    all_gather x6, waiting for transfers between devices, gather_rows(): return lax.all_gather(rows, 'dp', axis=0, tiled=True)  208 us
    all_to_all x1, blocking collectives, shards(): lax.all_to_all(partial, 'dp', split_axis=0, concat_axis=0, tiled=True)  55.4 us
    all_to_all x3, blocking collectives, to_tile(): out = lax.all_to_all(blocks, 'mp', split_axis=1, concat_axis=1, tiled=True)  42.9 us
    dot_general x10, matrix products, contract(): lax.dot_general(left, right, (((left_dim,), (right_dim,)), ((), ())), pre...  31.9 us
    all_to_all x2, waiting for transfers between devices, to_home(): all_to_all(jnp.stack(jnp.split(out, axis_size('mp'), axis=1), 0), 'mp', 0...  11 us
    all_to_all x1, waiting for transfers between devices, shards(): lax.all_to_all(slots, 'dp', split_axis=0, concat_axis=0, tiled=True)  10.1 us
    unnamed x45, local copies, waits for them, and re-layouts  9.22 us
  transfers between devices with their start and end apart: 11, of which 10 were waited for; matrix products, arithmetic and copies ran while one was open for 15% of the time, Pallas kernels for 0%

profile of v1, /device:TPU:0, one launch (start us, length us, event | category | flops | bytes accessed | tf_op | source)
XLA Modules:
  0.0 443.6 jit_solution(13945843990971652355)
XLA Ops:
  7.2 2.2 copy.152
  9.5 2.4 convolution_convert_fusion
  11.9 55.4 %all_to_all.50 = bf16[8,128,1024]{2,1,0:T(8,128)(2,1)} all-to-all(bf16[8,128,1024]{2,1,0:T(8,128)(2,1)S(1)} %bitcast.150), channel_id=1, replica_groups=mesh['dp'=8,'mp'=4] {'dp'}, dimensions={0} | all-to-all | bytes 4194304 | tf_op jit(solution)/shard_map/all_to_all | solution.py:66
  67.3 2.0 reduce_sum.39
  70.2 1.1 copy.122
  71.3 9.1 %all_to_all.51 = bf16[1,4,128,256]{3,2,0,1:T(8,128)(2,1)} all-to-all(bf16[1,4,128,256]{3,2,0,1:T(8,128)(2,1)S(1)} %copy.122), channel_id=1, replica_groups=mesh['dp'=8,'mp'=4] {'mp'}, dimensions={1} | all-to-all | bytes 524288 | tf_op jit(solution)/shard_map/all_to_all | solution.py:20
  80.4 1.8 copy.123
  82.6 1.2 copy.117
  83.8 1.2 copy.116
  85.2 16.9 %all_to_all.52 = bf16[4,4,128,256]{2,3,0,1:T(8,128)(2,1)S(1)} all-to-all(bf16[4,4,128,256]{2,3,0,1:T(8,128)(2,1)S(1)} %pad_maximum_fusion), channel_id=1, replica_groups=mesh['dp'=8,'mp'=4] {'mp'}, dimensions={1} | all-to-all | bytes 2097152 | tf_op jit(solution)/shard_map/all_to_all | solution.py:20
  104.8 1.2 copy.147
  106.1 24.6 %all-gather.9.cloned.1.call-done = bf16[1024,1024]{0,1:T(8,128)(2,1)} async-done(((bf16[128,1024]{0,1:T(8,128)(2,1)}), bf16[1024,1024]{0,1:T(8,128)(2,1)}) %all-gather.9.cloned.1.call-update) | async-done | bytes 2097168 | tf_op jit(solution)/shard_map/all_gather | solution.py:34
  130.7 3.4 fusion.85
  134.1 47.8 %all-gather.11.cloned.1.call-done = bf16[1024,1024]{0,1:T(8,128)(2,1)} async-done(((bf16[128,1024]{0,1:T(8,128)(2,1)}), bf16[1024,1024]{0,1:T(8,128)(2,1)}) %all-gather.11.cloned.1.call-update) | async-done | bytes 2097168 | tf_op jit(solution)/shard_map/all_gather | solution.py:34
  181.8 3.3 convolution_convert_fusion.3
  185.5 2.8 fusion.86
  188.2 44.8 %all-gather.7.cloned.1.call-done = bf16[1024,1024]{0,1:T(8,128)(2,1)} async-done(((bf16[128,1024]{0,1:T(8,128)(2,1)}), bf16[1024,1024]{0,1:T(8,128)(2,1)}) %all-gather.7.cloned.1.call-update) | async-done | bytes 2097168 | tf_op jit(solution)/shard_map/all_gather | solution.py:34
  233.0 3.1 convolution_convert_fusion.4
  236.2 1.2 copy.135
  237.4 1.2 copy.136
  238.8 17.0 %all_to_all.53 = f32[2,4,128,256]{2,3,0,1:T(8,128)S(1)} all-to-all(f32[2,4,128,256]{2,3,0,1:T(8,128)S(1)} %pad_maximum_fusion.1), channel_id=1, replica_groups=mesh['dp'=8,'mp'=4] {'mp'}, dimensions={1} | all-to-all | bytes 2097152 | tf_op jit(solution)/shard_map/all_to_all | solution.py:20
  257.1 4.8 %fusion.87 = (bf16[128,1024]{1,0:T(8,128)(2,1)}, f32[128,1024]{1,0:T(8,128)}) fusion(bf16[1024,1024]{0,1:T(8,128)(2,1)} %all-gather.11.cloned.1.call-done, bf16[1024,1024]{0,1:T(8,128)(2,1)} %all-gather.9.cloned.1.call-done, bf16[1024,1024]{0,1:T(8,128)(2,1)} %all-gather.7.cloned.1.call-done, s32[]{:T(128)S(6)} %select_n.28), kind=kOutput, calls=%fused_computation.120 | convolution fusion | flops 537133056 | bytes 5242884 | tf_op jit(solution)/shard_map/dot_general | solution.py:14
  261.9 3.1 convolution_convert_fusion.2
  265.1 3.5 all-to-all-start.7
  269.9 5.2 %all-to-all-done.7 = f32[8,1,256]{2,1,0:T(1,128)S(1)} async-done(((f32[8,1,256]{2,1,0:T(1,128)}), f32[8,1,256]{2,1,0:T(1,128)S(1)}, u32[]{:S(2)}, u32[]{:S(2)}) %all-to-all-start.7) | async-done | bytes 8224 | tf_op jit(solution)/shard_map/all_to_all | solution.py:115
  276.4 3.5 all-to-all-start.8
  279.9 3.1 all-gather.15.cloned.1.call-done
  283.1 2.1 fusion.2
  285.2 3.5 fusion.24
  288.9 43.8 %all-gather.13.cloned.1.call-done = bf16[1024,1024]{1,0:T(8,128)(2,1)} async-done(((bf16[128,1024]{1,0:T(8,128)(2,1)}), bf16[1024,1024]{1,0:T(8,128)(2,1)}) %all-gather.13.cloned.1.call-update) | async-done | bytes 2097168 | tf_op jit(solution)/shard_map/all_gather | solution.py:34
  332.7 2.1 fusion
  334.8 3.5 fusion.27
  338.5 44.4 %all-gather.17.cloned.1.call-done = bf16[1024,1024]{1,0:T(8,128)(2,1)} async-done(((bf16[128,1024]{1,0:T(8,128)(2,1)}), bf16[1024,1024]{1,0:T(8,128)(2,1)}) %all-gather.17.cloned.1.call-update) | async-done | bytes 2097168 | tf_op jit(solution)/shard_map/all_gather | solution.py:34
  382.9 2.1 convolution_convert_fusion.1
  386.3 3.6 all-to-all-start.5
  390.0 1.8 stack.88
  391.8 1.7 copy.124
  394.4 1.7 copy.126
  396.3 1.1 maximum_bitcast_fusion
  398.5 3.1 all-to-all-done.5
  401.6 4.2 all-to-all-start.3
  405.8 1.3 iota_compare_fusion.1
  407.0 1.4 iota_compare_fusion.3
  409.5 7.9 %all-to-all-done.3 = bf16[4,3,1,128,256]{4,3,2,1,0:T(8,128)(2,1)} async-done(((bf16[4,3,1,128,256]{4,3,2,1,0:T(8,128)(2,1)}), bf16[4,3,1,128,256]{4,3,2,1,0:T(8,128)(2,1)}, u32[]{:S(2)}, u32[]{:S(2)}) %all-to-all-start.3) | async-done | bytes 786464 | tf_op jit(solution)/shard_map/all_to_all | solution.py:29
  417.4 3.5 all-to-all-start.6
  421.0 1.4 convert_bitcast_fusion
  422.7 1.5 fusion.48
  425.3 10.1 %all-to-all-done.6 = bf16[8,128,256]{2,1,0:T(8,128)(2,1)S(1)} async-done(((bf16[8,128,256]{2,1,0:T(8,128)(2,1)}), bf16[8,128,256]{2,1,0:T(8,128)(2,1)S(1)}, u32[]{:S(2)}, u32[]{:S(2)}) %all-to-all-start.6) | async-done | bytes 524320 | tf_op jit(solution)/shard_map/all_to_all | solution.py:112
  (88 shorter events, 16.3 us)
Async XLA Ops:
  7.2 2.3 copy-start
  7.2 123.5 %all-gather.9.cloned.1.call-start = ((), (), s32[]{:S(2)}) async-start(), calls=%async_computation.10 | async-start | bytes 2359296 | tf_op jit(solution)/shard_map/all_gather | solution.py:34
  67.3 14.9 %copy-start.4 = (f32[4,128,256]{2,1,0:T(8,128)S(1)}, f32[4,128,256]{2,1,0:T(8,128)}, u32[]{:S(2)}) copy-start(f32[4,128,256]{2,1,0:T(8,128)} %param.19) | copy-start | bytes 1572868
  69.3 13.1 %copy-start.6 = (f32[4,128,256]{2,1,0:T(8,128)S(1)}, f32[4,128,256]{2,1,0:T(8,128)}, u32[]{:S(2)}) copy-start(f32[4,128,256]{2,1,0:T(8,128)} %param.18) | copy-start | bytes 1572868
  82.2 99.7 %all-gather.11.cloned.1.call-start = ((), (), s32[]{:S(2)}) async-start(), calls=%async_computation.11 | async-start | bytes 2359296 | tf_op jit(solution)/shard_map/all_gather | solution.py:34
  103.0 130.1 %all-gather.7.cloned.1.call-start = ((), (), s32[]{:S(2)}) async-start(), calls=%async_computation.9 | async-start | bytes 2359296 | tf_op jit(solution)/shard_map/all_gather | solution.py:34
  103.7 179.4 %all-gather.15.cloned.1.call-start = ((), (), s32[]{:S(2)}) async-start(), calls=%async_computation.13 | async-start | bytes 2359296 | tf_op jit(solution)/shard_map/all_gather | solution.py:34
  134.0 51.2 %copy-start.3 = (f32[1,128,4,256]{1,3,2,0:T(8,128)S(1)}, f32[1,128,4,256]{1,3,2,0:T(8,128)}, u32[]{:S(2)}) copy-start(f32[1,128,4,256]{1,3,2,0:T(8,128)} %get-tuple-element.17) | copy-start | bytes 1572868
  181.8 3.6 copy-start.1
  185.2 147.5 %all-gather.13.cloned.1.call-start = ((), (), s32[]{:S(2)}) async-start(), calls=%async_computation.12 | async-start | bytes 2359296 | tf_op jit(solution)/shard_map/all_gather | solution.py:34
  236.2 146.7 %all-gather.17.cloned.1.call-start = ((), (), s32[]{:S(2)}) async-start(), calls=%async_computation.14 | async-start | bytes 2359296 | tf_op jit(solution)/shard_map/all_gather | solution.py:34
  257.1 4.8 %copy-start.14 = (f32[128,1024]{1,0:T(8,128)S(1)}, f32[128,1024]{1,0:T(8,128)}, u32[]{:S(2)}) copy-start(f32[128,1024]{1,0:T(8,128)} %copy.148) | copy-start | bytes 1572868
  261.9 6.7 %copy-start.15 = (s32[5]{0:T(128)S(1)}, s32[5]{0:T(128)}, u32[]{:S(2)}) copy-start(s32[5]{0:T(128)} %param.15) | copy-start | bytes 64
  261.9 13.3 %copy-start.16 = (f32[256]{0:T(256)S(1)}, f32[256]{0:T(256)}, u32[]{:S(2)}) copy-start(f32[256]{0:T(256)} %param.23) | copy-start | bytes 3076
  261.9 13.3 %copy-start.17 = (f32[256]{0:T(256)S(1)}, f32[256]{0:T(256)}, u32[]{:S(2)}) copy-start(f32[256]{0:T(256)} %param.22) | copy-start | bytes 3076
  265.1 20.1 %copy-start.12 = (bf16[128,1024]{1,0:T(8,128)(2,1)S(1)}, bf16[128,1024]{1,0:T(8,128)(2,1)}, u32[]{:S(2)}) copy-start(bf16[128,1024]{1,0:T(8,128)(2,1)} %convolution_convert_fusion.3) | copy-start | bytes 786436
  265.1 10.1 %all-to-all-start.7 = ((f32[8,1,256]{2,1,0:T(1,128)}), f32[8,1,256]{2,1,0:T(1,128)S(1)}, u32[]{:S(2)}, u32[]{:S(2)}) async-start(f32[8,1,256]{2,1,0:T(1,128)} %bitcast.56), calls=%async_computation.7 | async-start | bytes 16384 | tf_op jit(solution)/shard_map/all_to_all | solution.py:115
  276.4 109.9 %all-to-all-start.8 = ((f32[8,1,256]{2,1,0:T(1,128)}), f32[8,1,256]{2,1,0:T(1,128)S(1)}, u32[]{:S(2)}, u32[]{:S(2)}) async-start(f32[8,1,256]{2,1,0:T(1,128)} %broadcast_select_fusion), calls=%async_computation.8 | async-start | bytes 16384 | tf_op jit(solution)/shard_map/all_to_all | solution.py:122
  288.6 46.1 %copy-start.13 = (bf16[128,1024]{1,0:T(8,128)(2,1)S(1)}, bf16[128,1024]{1,0:T(8,128)(2,1)}, u32[]{:S(2)}) copy-start(bf16[128,1024]{1,0:T(8,128)(2,1)} %convolution_convert_fusion.4) | copy-start | bytes 786436
  334.8 48.1 %copy-start.2 = (bf16[1,128,4,256]{1,3,2,0:T(8,128)(2,1)S(1)}, bf16[1,128,4,256]{1,3,2,0:T(8,128)(2,1)}, u32[]{:S(2)}) copy-start(bf16[1,128,4,256]{1,3,2,0:T(8,128)(2,1)} %get-tuple-element.21) | copy-start | bytes 786436
  385.3 8.2 %copy-start.10 = (bf16[128,1024]{1,0:T(8,128)(2,1)S(1)}, bf16[128,1024]{1,0:T(8,128)(2,1)}, u32[]{:S(2)}) copy-start(bf16[128,1024]{1,0:T(8,128)(2,1)} %get-tuple-element.42) | copy-start | bytes 786436
  386.3 9.7 %copy-start.11 = (bf16[128,1024]{1,0:T(8,128)(2,1)S(1)}, bf16[128,1024]{1,0:T(8,128)(2,1)}, u32[]{:S(2)}) copy-start(bf16[128,1024]{1,0:T(8,128)(2,1)} %get-tuple-element.44) | copy-start | bytes 786436
  386.3 15.2 %all-to-all-start.5 = ((bf16[4,3,1,128,256]{4,3,2,1,0:T(8,128)(2,1)}), bf16[4,3,1,128,256]{4,3,2,1,0:T(8,128)(2,1)S(1)}, u32[]{:S(2)}, u32[]{:S(2)}) async-start(bf16[4,3,1,128,256]{4,3,2,1,0:T(8,128)(2,1)} %pad_maximum_fusion.3), calls=%async_computation.5 | async-start | bytes 1572864 | tf_op jit(solution)/shard_map/all_to_all | solution.py:29
  401.6 15.9 %all-to-all-start.3 = ((bf16[4,3,1,128,256]{4,3,2,1,0:T(8,128)(2,1)}), bf16[4,3,1,128,256]{4,3,2,1,0:T(8,128)(2,1)}, u32[]{:S(2)}, u32[]{:S(2)}) async-start(bf16[4,3,1,128,256]{4,3,2,1,0:T(8,128)(2,1)} %pad_maximum_fusion.2), calls=%async_computation.3 | async-start | bytes 1572864 | tf_op jit(solution)/shard_map/all_to_all | solution.py:29
  417.4 17.9 %all-to-all-start.6 = ((bf16[8,128,256]{2,1,0:T(8,128)(2,1)}), bf16[8,128,256]{2,1,0:T(8,128)(2,1)S(1)}, u32[]{:S(2)}, u32[]{:S(2)}) async-start(bf16[8,128,256]{2,1,0:T(8,128)(2,1)} %select_select_fusion), calls=%async_computation.6 | async-start | bytes 1048576 | tf_op jit(solution)/shard_map/all_to_all | solution.py:112
  421.0 1.5 copy-start.5
  421.0 1.5 copy-start.7
  421.0 1.6 copy-start.8
  421.0 1.7 copy-start.9
Sparse Core Ops, SparseCore 0:
  82.3 48.3 all-gather.8
  133.3 48.5 all-gather.10
  184.5 48.5 all-gather.6
  235.6 47.4 all-gather.14
  285.0 47.5 all-gather.12
  335.2 47.6 all-gather.16
